TPU v7x, 512 devices: a whole 4x4x16 slice. The times are simulated.
512 devices in a mesh: fsdp: 32 (over x, z_lo), member: 16 (over y, z_hi, core).
Axes of the slice: x: 4, y: 4, z: 16 (z_hi: 2, z_lo: 8; z = z_hi * 8 + z_lo), core: 2. Of those that a mesh axis runs over, the one named last changes fastest.
Arguments:
- frames: bfloat16 [16, 4608, 1536], P('member', 'fsdp'), may hold values from -6 to 6
- layer_norm_gain: float32 [1536], replicated, may hold values from 0.25 to 1.75
- input_projection: bfloat16 [1536, 6144], P('fsdp', 'member'), may hold values from -0.15625 to 0.15625
- output_projection: bfloat16 [6144, 1536], P('member', 'fsdp'), may hold values from -0.078125 to 0.078125
- adapter_down_map: bfloat16 [16, 1536, 64], P('member'), may hold values from -0.15625 to 0.15625
- adapter_up_map: bfloat16 [16, 64, 6144], P('member'), may hold values from -0.75 to 0.75
- lengths: int32 [16, 32], P('member', 'fsdp'), may hold values from 90 to 126, as said below
- cotangent: bfloat16 [16, 4608, 1536], P('member', 'fsdp'), may hold values from -0.29882812 to 0.29882812
Outputs:
- down_map_gradient: float32 [16, 1536, 64], P('member')
- up_map_gradient: float32 [16, 64, 6144], P('member')
Inputs may be any that keep to these rules, and one draw needn't show every extreme that they name: `lengths`: each member has at least one utterance of exactly 126 frames.
All inputs are finite; a program needn't handle non-finite values.
Results may differ from a plain program's by a relative error of at most 0.0058.
Values may be sent and summed in bfloat16 or wider, within the bound.
A program may use at most 128 MiB of HBM per device.

v0:
```python
import jax
import jax.numpy as jnp
from jax import lax
from jax.sharding import PartitionSpec as P

BUCKET = 144


def on_device(
    frames,
    layer_norm_gain,
    input_projection,
    output_projection,
    adapter_down_map,
    adapter_up_map,
    lengths,
    cotangent,
):
    members = lax.axis_size("member")
    values = frames[0].astype(jnp.float32)
    mean = jnp.mean(values, axis=1, keepdims=True)
    var = jnp.mean((values - mean) ** 2, axis=1, keepdims=True)
    normed_input = (layer_norm_gain * (values - mean) / jnp.sqrt(var + 1e-05)).astype(jnp.bfloat16)
    low_rank_state = jnp.dot(
        normed_input, adapter_down_map[0], preferred_element_type=jnp.float32
    ).astype(jnp.bfloat16)
    positions = jnp.arange(BUCKET, dtype=jnp.int32)
    mask = (positions[None, :] < lengths[0][:, None]).reshape(-1)
    masked = cotangent[0] * mask.astype(cotangent.dtype)[:, None]
    rows = normed_input.shape[0]
    up_map_slices = lax.all_to_all(
        adapter_up_map, "member", split_axis=2, concat_axis=0, tiled=True
    )
    stacked_norm, stacked_low, stacked_grad = (
        lax.all_gather(normed_input, "member", axis=0, tiled=True),
        lax.all_gather(low_rank_state, "member", axis=0, tiled=True),
        lax.all_gather(masked, "member", axis=0, tiled=True),
    )
    low_rank_blocks = stacked_low.reshape(members, rows, -1)
    adapter_term = jnp.einsum(
        "dgs,dsb->dgb", low_rank_blocks, up_map_slices, preferred_element_type=jnp.float32
    )
    adapter_term = adapter_term.reshape(members * rows, -1)
    columns = stacked_norm
    pre = adapter_term + jnp.dot(
        columns,
        lax.all_gather(input_projection, "fsdp", axis=0, tiled=True),
        preferred_element_type=jnp.float32,
    )
    columns = stacked_grad
    dhid = 0.5 * lax.dot_general(
        columns,
        lax.all_gather(output_projection, "fsdp", axis=1, tiled=True),
        (((1,), (1,)), ((), ())),
        preferred_element_type=jnp.float32,
    )
    sigma = jax.nn.sigmoid(pre)
    dpre = (dhid * sigma * (1.0 + pre * (1.0 - sigma))).astype(jnp.bfloat16)
    preact_gradient_blocks = dpre.reshape(members, rows, -1)
    up_partial = jnp.einsum(
        "jnz,jnv->jzv", low_rank_blocks, preact_gradient_blocks, preferred_element_type=jnp.float32
    )
    back_partial = jnp.einsum(
        "yha,ywa->yhw", preact_gradient_blocks, up_map_slices, preferred_element_type=jnp.float32
    )
    back = lax.psum_scatter(back_partial, "member", scatter_dimension=0, tiled=True)[0].astype(
        jnp.bfloat16
    )
    down_partial = jnp.dot(normed_input.T, back, preferred_element_type=jnp.float32)
    up_summed = lax.psum(up_partial, "fsdp")
    up_map_gradient = lax.all_to_all(up_summed, "member", split_axis=0, concat_axis=2, tiled=True)
    down_map_gradient = lax.psum(down_partial, "fsdp")
    return (down_map_gradient[None], up_map_gradient)


def solution(mesh):
    in_specs = (
        P("member", "fsdp", None),
        P(),
        P("fsdp", "member"),
        P("member", "fsdp"),
        P("member", None, None),
        P("member", None, None),
        P("member", "fsdp"),
        P("member", "fsdp", None),
    )
    out_specs = (P("member", None, None), P("member", None, None))
    return jax.shard_map(
        on_device, mesh=mesh, in_specs=in_specs, out_specs=out_specs, check_vma=False
    )
```

profile of v0, /device:TPU:1, one launch (start us, length us, event | category | flops | bytes accessed | tf_op | source)
XLA Modules:
  0.0 1449.9 jit_solution(2812259246271979070)
XLA Ops:
  9.1 1.3 fusion.10
  10.4 2.0 fusion.12
  13.9 1.9 bitcast_multiply_fusion
  15.8 6.7 copy.12
  23.0 34.4 %reduce.1 = bf16[6144,64]{1,0:T(8,128)(2,1)} reduce(bf16[6144,1,64]{2,1,0:T(2,128)(2,1)S(1)} %bitcast.57, bf16[]{:T(256)} %broadcast.58), dimensions={1}, to_apply=%bitcast.44.reduce_sub_computation | reduce | bytes 1572866
  57.5 3.9 reshape.87
  61.4 19.2 %all-to-all-start = ((bf16[16,2,12288]{2,1,0:T(2,128)(2,1)}), bf16[16,2,12288]{2,1,0:T(2,128)(2,1)}, u32[]{:S(2)}, u32[]{:S(2)}) async-start(bf16[16,2,12288]{2,1,0:T(2,128)(2,1)} %reshape.87), calls=%async_computation | async-start | bytes 1572864 | tf_op jit(solution)/shard_map/all_to_all | solution.py:31
  81.9 75.8 %all-gather = bf16[16,144,64]{1,2,0:T(8,128)(2,1)} all-gather(bf16[1,144,64]{1,2,0:T(8,128)(2,1)S(1)} %fusion.3), channel_id=1, replica_groups=mesh['fsdp'=32,'member'=16] {'member'}, dimensions={0}, use_global_device_ids=true | all-gather | bytes 313344 | tf_op jit(solution)/shard_map/all_gather | solution.py:36
  157.8 4.6 reshape.88
  162.3 1.3 copy.18
  163.7 1.7 copy.14
  165.4 3.5 fusion.15
  168.9 70.4 %all-gather.12.cloned.1.call-done = bf16[1536,384]{1,0:T(8,128)(2,1)} async-done(((bf16[48,384]{1,0:T(8,128)(2,1)}), bf16[1536,384]{1,0:T(8,128)(2,1)}) %all-gather.12.cloned.1.call-update) | async-done | bytes 1179664 | tf_op jit(solution)/shard_map/all_gather | solution.py:47
  239.3 179.4 %all-gather.10.cloned.1.call-done = bf16[2304,1536]{1,0:T(8,128)(2,1)} async-done(((bf16[144,1536]{1,0:T(8,128)(2,1)}), bf16[2304,1536]{1,0:T(8,128)(2,1)}) %all-gather.10.cloned.1.call-update) | async-done | bytes 7077904 | tf_op jit(solution)/shard_map/all_gather | solution.py:35
  418.7 10.0 convolution_add_fusion
  428.7 184.5 %all-gather.8.cloned.1.call-done = bf16[384,1536]{0,1:T(8,128)(2,1)} async-done(((bf16[384,48]{0,1:T(8,128)(2,1)}), bf16[384,1536]{0,1:T(8,128)(2,1)}) %all-gather.8.cloned.1.call-update) | async-done | bytes 1179664 | tf_op jit(solution)/shard_map/all_gather | solution.py:53
  613.2 183.5 %all-gather.6.cloned.1.call-done = bf16[2304,1536]{1,0:T(8,128)(2,1)} async-done(((bf16[144,1536]{1,0:T(8,128)(2,1)}), bf16[2304,1536]{1,0:T(8,128)(2,1)}) %all-gather.6.cloned.1.call-update) | async-done | bytes 7077904 | tf_op jit(solution)/shard_map/all_gather | solution.py:37
  796.6 9.0 fusion.2
  805.6 1.9 fusion.13
  807.6 1.6 fusion.21
  809.2 94.6 %reduce-scatter.2.cloned.1.call-done = f32[1,144,64]{1,2,0:T(8,128)} async-done(((f32[16,144,64]{1,2,0:T(8,128)}), f32[1,144,64]{1,2,0:T(8,128)}) %reduce-scatter.2.cloned.1.call-update) | async-done | bytes 36880 | tf_op jit(solution)/shard_map/reduce_scatter | solution.py:66
  903.9 1.8 convolution_bitcast_fusion
  905.7 434.8 %all-reduce.3.cloned.1.call-done = (f32[1,1536,64]{1,2,0:T(8,128)}, f32[16,64,384]{2,1,0:T(8,128)}) async-done(((f32[1,1536,64]{1,2,0:T(8,128)}, f32[16,64,384]{2,1,0:T(8,128)}), (f32[1,1536,64]{1,2,0:T(8,128)}, f32[16,64,384]{2,1,0:T(8,128)})) %all-reduce.3.cloned.1.call-update) | async-done | bytes 1966096 | tf_op jit(solution)/shard_map/psum | solution.py:72
  1340.4 100.6 %all_to_all.36 = f32[16,64,384]{2,1,0:T(8,128)S(1)} all-to-all(f32[16,64,384]{2,1,0:T(8,128)} %get-tuple-element.3), channel_id=1, replica_groups=mesh['fsdp'=32,'member'=16] {'member'}, dimensions={0} | all-to-all | bytes 3145728 | tf_op jit(solution)/shard_map/all_to_all | solution.py:71
  (36 shorter events, 6.6 us)
Async XLA Ops:
  7.2 74.5 %copy-start = (bf16[1,1536,64]{1,2,0:T(8,128)(2,1)S(1)}, bf16[1,1536,64]{1,2,0:T(8,128)(2,1)}, u32[]{:S(2)}) copy-start(bf16[1,1536,64]{1,2,0:T(8,128)(2,1)} %param.12) | copy-start | bytes 589828
  7.2 232.1 %all-gather.12.cloned.1.call-start = ((), (), s32[]{:S(2)}) async-start(), calls=%async_computation.6 | async-start | bytes 1216512 | tf_op jit(solution)/shard_map/all_gather | solution.py:47
  7.9 410.8 %all-gather.10.cloned.1.call-start = ((), (), s32[]{:S(2)}) async-start(), calls=%async_computation.5 | async-start | bytes 7520256 | tf_op jit(solution)/shard_map/all_gather | solution.py:35
  12.5 600.7 %all-gather.8.cloned.1.call-start = ((), (), s32[]{:S(2)}) async-start(), calls=%async_computation.4 | async-start | bytes 1216512 | tf_op jit(solution)/shard_map/all_gather | solution.py:53
  13.2 783.4 %all-gather.6.cloned.1.call-start = ((), (), s32[]{:S(2)}) async-start(), calls=%async_computation.3 | async-start | bytes 7520256 | tf_op jit(solution)/shard_map/all_gather | solution.py:37
  23.0 57.6 %copy-start.6 = (f32[1536]{0:T(1024)S(1)}, f32[1536]{0:T(1024)}, u32[]{:S(2)}) copy-start(f32[1536]{0:T(1024)} %param.9) | copy-start | bytes 18436
  57.5 23.2 %copy-start.1 = (bf16[1,144,1536]{2,1,0:T(8,128)(2,1)S(1)}, bf16[1,144,1536]{2,1,0:T(8,128)(2,1)}, u32[]{:S(2)}) copy-start(bf16[1,144,1536]{2,1,0:T(8,128)(2,1)} %param.8) | copy-start | bytes 1327108
  61.4 96.4 %all-to-all-start = ((bf16[16,2,12288]{2,1,0:T(2,128)(2,1)}), bf16[16,2,12288]{2,1,0:T(2,128)(2,1)}, u32[]{:S(2)}, u32[]{:S(2)}) async-start(bf16[16,2,12288]{2,1,0:T(2,128)(2,1)} %reshape.87), calls=%async_computation | async-start | bytes 1572864 | tf_op jit(solution)/shard_map/all_to_all | solution.py:31
  80.6 823.2 %reduce-scatter.2.cloned.1.call-start = ((), (), s32[]{:S(2)}) async-start(), calls=%async_computation.7 | async-start | bytes 1114112 | tf_op jit(solution)/shard_map/reduce_scatter | solution.py:66
  80.9 0.8 copy-start.3
  805.6 2.0 copy-start.2
  807.5 96.3 %copy-start.4 = (bf16[144,1536]{1,0:T(8,128)(2,1)S(1)}, bf16[144,1536]{1,0:T(8,128)(2,1)}, u32[]{:S(2)}) copy-start(bf16[144,1536]{1,0:T(8,128)(2,1)} %copy-done.3) | copy-start | bytes 1327108
  807.5 532.9 %all-reduce.3.cloned.1.call-start = ((), (), s32[]{:S(2)}) async-start(), calls=%async_computation.8 | async-start | bytes 3932160 | tf_op jit(solution)/shard_map/psum | solution.py:72
  1340.4 101.8 %copy-start.5 = (f32[1,1536,64]{1,2,0:T(8,128)S(1)}, f32[1,1536,64]{1,2,0:T(8,128)}, u32[]{:S(2)}) copy-start(f32[1,1536,64]{1,2,0:T(8,128)} %get-tuple-element.4) | copy-start | bytes 1179652
Sparse Core Ops, SparseCore 0:
  10.1 229.1 all-gather.11
  242.5 176.1 all-gather.9
  420.8 192.3 all-gather.7
  616.3 180.3 all-gather.5
  807.7 96.1 reduce-scatter.1
  907.6 432.8 all-reduce.2
where the time goes:
time: 1450 us
  waiting for transfers between devices  1150 us (79%)
  blocking collectives  176 us (12%)
  other arithmetic  41.1 us (3%)
  matrix products  28 us (2%)
  local copies, waits for them, and re-layouts  21.5 us (1%)
  starting transfers between devices  19.5 us (1%)
  between operations  14.9 us (1%)
    psum x1, waiting for transfers between devices, on_device(): down_map_gradient = lax.psum(down_partial, 'fsdp')  435 us
    all_gather x1, waiting for transfers between devices, on_device(): lax.all_gather(output_projection, 'fsdp', axis=1, tiled=True)  184 us
    all_gather x1, waiting for transfers between devices, on_device(): lax.all_gather(masked, 'member', axis=0, tiled=True)  183 us
    all_gather x1, waiting for transfers between devices, on_device(): lax.all_gather(normed_input, 'member', axis=0, tiled=True)  179 us
    all_to_all x1, blocking collectives, on_device(): lax.all_to_all(up_summed, 'member', split_axis=0, concat_axis=2, tiled=True)  101 us
    reduce_scatter x1, waiting for transfers between devices, on_device(): lax.psum_scatter(back_partial, 'member', scatter_dimension=0, tiled=True)[0]  94.6 us
    all_gather x1, blocking collectives, on_device(): lax.all_gather(low_rank_state, 'member', axis=0, tiled=True)  75.8 us
    all_gather x1, waiting for transfers between devices, on_device(): lax.all_gather(input_projection, 'fsdp', axis=0, tiled=True)  70.4 us
  transfers between devices with their start and end apart: 7, of which 6 were waited for; matrix products, arithmetic and copies ran while one was open for 5% of the time, Pallas kernels for 0%

commit v1 on v0

--- a/solution.py
+++ b/solution.py
@@ -69,7 +69,7 @@
     down_partial = jnp.dot(normed_input.T, back, preferred_element_type=jnp.float32)
     up_summed = lax.psum(up_partial, "fsdp")
     up_map_gradient = lax.all_to_all(up_summed, "member", split_axis=0, concat_axis=2, tiled=True)
-    down_map_gradient = lax.psum(down_partial, "fsdp")
+    down_map_gradient = jnp.sum(lax.all_gather(down_partial, "fsdp"), axis=0)
     return (down_map_gradient[None], up_map_gradient)
 
 

time: 1450 us -> 1730 us (1.19)
  waiting for transfers between devices: 1150 us -> 1390 us
  blocking collectives: 176 us -> 194 us
    all_gather x0 -> x1, waiting for transfers between devices: none -> 242 us  [on_device(): down_map_gradient = jnp.sum(lax.all_gather(down_partial, 'fsdp'), axis=0)]
    all_to_all x1, blocking collectives: 101 us -> 118 us  [on_device(): lax.all_to_all(up_summed, 'member', split_axis=0, concat_axis=2, tiled=True)]
  transfers between devices with their start and end apart: 7 -> 8, of which waited for: 6 -> 7; matrix products, arithmetic and copies ran while one was open for 5% -> 5% of each run, Pallas kernels for 0% -> 0%
where the time goes in v1:
time: 1730 us
  waiting for transfers between devices  1390 us (80%)
  blocking collectives  194 us (11%)
  other arithmetic  48.5 us (3%)
  local copies, waits for them, and re-layouts  36.9 us (2%)
  matrix products  28 us (2%)
  starting transfers between devices  19.5 us (1%)
    psum x1, waiting for transfers between devices, on_device(): up_summed = lax.psum(up_partial, 'fsdp')  434 us
    all_gather x1, waiting for transfers between devices, on_device(): down_map_gradient = jnp.sum(lax.all_gather(down_partial, 'fsdp'), axis=0)  242 us
    all_gather x1, waiting for transfers between devices, on_device(): lax.all_gather(output_projection, 'fsdp', axis=1, tiled=True)  184 us
    all_gather x1, waiting for transfers between devices, on_device(): lax.all_gather(masked, 'member', axis=0, tiled=True)  183 us
    all_gather x1, waiting for transfers between devices, on_device(): lax.all_gather(normed_input, 'member', axis=0, tiled=True)  182 us
    all_to_all x1, blocking collectives, on_device(): lax.all_to_all(up_summed, 'member', split_axis=0, concat_axis=2, tiled=True)  118 us
    reduce_scatter x1, waiting for transfers between devices, on_device(): lax.psum_scatter(back_partial, 'member', scatter_dimension=0, tiled=True)[0]  94.5 us
    all_gather x1, blocking collectives, on_device(): lax.all_gather(low_rank_state, 'member', axis=0, tiled=True)  75.8 us
  transfers between devices with their start and end apart: 8, of which 7 were waited for; matrix products, arithmetic and copies ran while one was open for 5% of the time, Pallas kernels for 0%

profile of v1, /device:TPU:1, one launch (start us, length us, event | category | flops | bytes accessed | tf_op | source)
XLA Modules:
  0.0 1733.2 jit_solution(4648620251917834198)
XLA Ops:
  10.4 2.0 fusion.12
  13.9 1.9 bitcast_multiply_fusion
  15.8 6.7 copy.12
  23.0 34.4 %reduce.1 = bf16[6144,64]{1,0:T(8,128)(2,1)} reduce(bf16[6144,1,64]{2,1,0:T(2,128)(2,1)S(1)} %bitcast.62, bf16[]{:T(256)} %broadcast.58), dimensions={1}, to_apply=%bitcast.48.reduce_sub_computation | reduce | bytes 1572866
  57.5 3.9 reshape.88
  61.4 19.2 %all-to-all-start = ((bf16[16,2,12288]{2,1,0:T(2,128)(2,1)}), bf16[16,2,12288]{2,1,0:T(2,128)(2,1)}, u32[]{:S(2)}, u32[]{:S(2)}) async-start(bf16[16,2,12288]{2,1,0:T(2,128)(2,1)} %reshape.88), calls=%async_computation | async-start | bytes 1572864 | tf_op jit(solution)/shard_map/all_to_all | solution.py:31
  81.9 75.8 %all-gather.1 = bf16[16,144,64]{1,2,0:T(8,128)(2,1)} all-gather(bf16[1,144,64]{1,2,0:T(8,128)(2,1)S(1)} %fusion.3), channel_id=1, replica_groups=mesh['fsdp'=32,'member'=16] {'member'}, dimensions={0}, use_global_device_ids=true | all-gather | bytes 313344 | tf_op jit(solution)/shard_map/all_gather | solution.py:36
  157.7 4.6 reshape.89
  163.6 1.7 copy.14
  165.3 3.5 fusion.15
  168.8 69.3 %all-gather.14.cloned.1.call-done = bf16[1536,384]{1,0:T(8,128)(2,1)} async-done(((bf16[48,384]{1,0:T(8,128)(2,1)}), bf16[1536,384]{1,0:T(8,128)(2,1)}) %all-gather.14.cloned.1.call-update) | async-done | bytes 1179664 | tf_op jit(solution)/shard_map/all_gather | solution.py:47
  238.1 181.8 %all-gather.12.cloned.1.call-done = bf16[2304,1536]{1,0:T(8,128)(2,1)} async-done(((bf16[144,1536]{1,0:T(8,128)(2,1)}), bf16[2304,1536]{1,0:T(8,128)(2,1)}) %all-gather.12.cloned.1.call-update) | async-done | bytes 7077904 | tf_op jit(solution)/shard_map/all_gather | solution.py:35
  419.8 10.0 convolution_add_fusion
  429.8 184.5 %all-gather.10.cloned.1.call-done = bf16[384,1536]{0,1:T(8,128)(2,1)} async-done(((bf16[384,48]{0,1:T(8,128)(2,1)}), bf16[384,1536]{0,1:T(8,128)(2,1)}) %all-gather.10.cloned.1.call-update) | async-done | bytes 1179664 | tf_op jit(solution)/shard_map/all_gather | solution.py:53
  614.3 183.5 %all-gather.8.cloned.1.call-done = bf16[2304,1536]{1,0:T(8,128)(2,1)} async-done(((bf16[144,1536]{1,0:T(8,128)(2,1)}), bf16[2304,1536]{1,0:T(8,128)(2,1)}) %all-gather.8.cloned.1.call-update) | async-done | bytes 7077904 | tf_op jit(solution)/shard_map/all_gather | solution.py:37
  797.8 9.0 fusion.2
  806.8 1.9 fusion.13
  810.4 94.5 %reduce-scatter.2.cloned.1.call-done = f32[1,144,64]{1,2,0:T(8,128)} async-done(((f32[16,144,64]{1,2,0:T(8,128)}), f32[1,144,64]{1,2,0:T(8,128)}) %reduce-scatter.2.cloned.1.call-update) | async-done | bytes 36880 | tf_op jit(solution)/shard_map/reduce_scatter | solution.py:66
  904.9 1.8 fusion.19
  906.8 433.9 %all-reduce.2.cloned.1.call-done = f32[16,64,384]{2,1,0:T(8,128)} async-done(((f32[16,64,384]{2,1,0:T(8,128)}), f32[16,64,384]{2,1,0:T(8,128)}) %all-reduce.2.cloned.1.call-update) | async-done | bytes 1572880 | tf_op jit(solution)/shard_map/psum | solution.py:70
  1340.6 118.5 %all_to_all.36 = f32[16,64,384]{2,1,0:T(8,128)S(1)} all-to-all(f32[16,64,384]{2,1,0:T(8,128)} %all-reduce.2.cloned.1.call-done), channel_id=1, replica_groups=mesh['fsdp'=32,'member'=16] {'member'}, dimensions={0} | all-to-all | bytes 3145728 | tf_op jit(solution)/shard_map/all_to_all | solution.py:71
  1460.4 242.4 %all-gather.16.cloned.1.call-done = f32[49152,64]{0,1:T(8,128)} async-done(((f32[1536,64]{0,1:T(8,128)}), f32[49152,64]{0,1:T(8,128)}) %all-gather.16.cloned.1.call-update) | async-done | bytes 12582928 | tf_op jit(solution)/shard_map/all_gather | solution.py:72
  1702.7 16.2 copy.20
  1718.9 7.5 bitcast_reduce_fusion
  (40 shorter events, 10.2 us)
Async XLA Ops:
  7.2 74.5 %copy-start = (bf16[1,1536,64]{1,2,0:T(8,128)(2,1)S(1)}, bf16[1,1536,64]{1,2,0:T(8,128)(2,1)}, u32[]{:S(2)}) copy-start(bf16[1,1536,64]{1,2,0:T(8,128)(2,1)} %param.12) | copy-start | bytes 589828
  7.2 230.9 %all-gather.14.cloned.1.call-start = ((), (), s32[]{:S(2)}) async-start(), calls=%async_computation.6 | async-start | bytes 1216512 | tf_op jit(solution)/shard_map/all_gather | solution.py:47
  7.9 411.9 %all-gather.12.cloned.1.call-start = ((), (), s32[]{:S(2)}) async-start(), calls=%async_computation.5 | async-start | bytes 7520256 | tf_op jit(solution)/shard_map/all_gather | solution.py:35
  12.4 601.8 %all-gather.10.cloned.1.call-start = ((), (), s32[]{:S(2)}) async-start(), calls=%async_computation.4 | async-start | bytes 1216512 | tf_op jit(solution)/shard_map/all_gather | solution.py:53
  13.2 784.6 %all-gather.8.cloned.1.call-start = ((), (), s32[]{:S(2)}) async-start(), calls=%async_computation.3 | async-start | bytes 7520256 | tf_op jit(solution)/shard_map/all_gather | solution.py:37
  23.0 57.6 %copy-start.6 = (f32[1536]{0:T(1024)S(1)}, f32[1536]{0:T(1024)}, u32[]{:S(2)}) copy-start(f32[1536]{0:T(1024)} %param.9) | copy-start | bytes 18436
  57.5 23.2 %copy-start.2 = (bf16[1,144,1536]{2,1,0:T(8,128)(2,1)S(1)}, bf16[1,144,1536]{2,1,0:T(8,128)(2,1)}, u32[]{:S(2)}) copy-start(bf16[1,144,1536]{2,1,0:T(8,128)(2,1)} %param.8) | copy-start | bytes 1327108
  61.4 96.3 %all-to-all-start = ((bf16[16,2,12288]{2,1,0:T(2,128)(2,1)}), bf16[16,2,12288]{2,1,0:T(2,128)(2,1)}, u32[]{:S(2)}, u32[]{:S(2)}) async-start(bf16[16,2,12288]{2,1,0:T(2,128)(2,1)} %reshape.88), calls=%async_computation | async-start | bytes 1572864 | tf_op jit(solution)/shard_map/all_to_all | solution.py:31
  80.6 824.4 %reduce-scatter.2.cloned.1.call-start = ((), (), s32[]{:S(2)}) async-start(), calls=%async_computation.7 | async-start | bytes 1114112 | tf_op jit(solution)/shard_map/reduce_scatter | solution.py:66
  80.9 0.7 copy-start.4
  806.8 1.9 copy-start.3
  808.6 96.3 %copy-start.5 = (bf16[144,1536]{1,0:T(8,128)(2,1)S(1)}, bf16[144,1536]{1,0:T(8,128)(2,1)}, u32[]{:S(2)}) copy-start(bf16[144,1536]{1,0:T(8,128)(2,1)} %copy-done.4) | copy-start | bytes 1327108
  808.7 532.0 %all-reduce.2.cloned.1.call-start = ((), (), s32[]{:S(2)}) async-start(), calls=%async_computation.8 | async-start | bytes 3145728 | tf_op jit(solution)/shard_map/psum | solution.py:70
  810.4 892.4 %all-gather.16.cloned.1.call-start = ((), (), s32[]{:S(2)}) async-start(), calls=%async_computation.9 | async-start | bytes 12976128 | tf_op jit(solution)/shard_map/all_gather | solution.py:72
  1702.7 23.7 %copy-start.1 = (bf16[1,1536,64]{1,2,0:T(8,128)(2,1)S(1)}, bf16[1,1536,64]{1,2,0:T(8,128)(2,1)}, u32[]{:S(2)}) copy-start(bf16[1,1536,64]{1,2,0:T(8,128)(2,1)} %param.12) | copy-start | bytes 589828
Sparse Core Ops, SparseCore 0:
  10.1 227.9 all-gather.13
  241.3 178.4 all-gather.11
  421.9 192.3 all-gather.9
  617.4 180.3 all-gather.7
  808.8 96.1 reduce-scatter.1
  908.5 432.0 all-reduce.1
  1343.3 359.3 all-gather.15
